TPU v7x, 32 devices: a whole 2x2x4 slice. The times are simulated.
32 devices in a mesh: groups: 2 (over y), tile: 4 (over z), sub: 2 (over x), rep: 2 (over core).
Axes of the slice: x: 2, y: 2, z: 4, core: 2. Of those that a mesh axis runs over, the one named last changes fastest.
Arguments:
- pressure: float32 [64, 32, 256], P(('groups', 'tile'), 'sub', 'rep'), parts along dimension 0, may hold values from -3 to 3
- previous_pressure: float32 [64, 32, 256], P(('groups', 'tile'), 'sub', 'rep'), parts along dimension 0, may hold values from -3 to 3
- courant_square: float32 [64, 32, 256], P(('groups', 'tile'), 'sub', 'rep'), parts along dimension 0, may hold values from 0.07 to 0.22
- node_area: float32 [12288], P(('groups', 'tile', 'sub', 'rep')), parts along dimension 0, may hold values from 0.25 to 4
- mode_shapes: bfloat16 [12288, 2048], P(('groups', 'tile', 'sub', 'rep')), parts along dimension 0, may hold values from -0.049804688 to 0.049804688
- frequency: float32 [4096], P('groups'), parts along dimension 0, may hold values from 0.4 to 1.3
- damping_ratio: float32 [4096], P('groups'), parts along dimension 0, may hold values from 0.02 to 0.4
- modal_start: float32 [2, 4096], P(None, 'groups'), parts along dimension 1, may hold values from -4 to 4
- slot_cell: int32 [8, 2, 2, 384], P(('groups', 'tile'), 'sub', 'rep'), parts along dimension 0, may hold values from 0 to 16383, as said below
- slot_owner: int32 [8, 2, 2, 384, 1], P(('groups', 'tile'), 'sub', 'rep'), parts along dimension 0, may hold values from 0 to 3; in each aligned block of 384 rows (0 to 383, 384 to 767, ..., all dimensions but the last counted through in order) at most 96 rows name the same one
- surface_count: int32 [4, 2, 4], P(('groups', 'sub'), 'rep', 'tile'), parts along dimension 0, may hold values from 1 to 384, 512 in all within a row
Outputs:
- final_pressure: float32 [64, 32, 256], P(('groups', 'tile'), 'sub', 'rep'), parts along dimension 0
- prior_pressure: float32 [64, 32, 256], P(('groups', 'tile'), 'sub', 'rep'), parts along dimension 0
- surface_accel: bfloat16 [8, 2, 2, 4, 384], P(('groups', 'tile'), 'sub', 'rep'), parts along dimension 0
- modal_state: float32 [2, 4096], P(None, ('groups', 'tile', 'sub', 'rep')), parts along dimension 1
There are 2 independent parts, one for each index of `groups`. A program takes and returns all parts, laid end to end along the dimension named above; each array names one. Nothing has to cross between parts.
Inputs may be any that keep to these rules, and one draw needn't show every extreme that they name: `slot_cell`: slot j of a block lies in the block's cells j * (42) to (j + 1) (42) - 1, so a block's slots name distinct cells. `slot_owner`: every owner index is named by exactly 96 of the 384 slots of each block (t, s, r). `surface_count`: for fixed s and r the counts over t sum to 128 times the number of tile indices, and one of them equals 384.
All inputs are finite; a program needn't handle non-finite values. No bound on the sum of `surface_count` on one device may be relied on, other than what follows from the above.
Results may differ from a plain program's by a relative error of at most 0.0098.
Values may be sent and summed in bfloat16 or wider, within the bound.
A program may use at most 64 MiB of HBM per device.

v0:
```python
import jax
import jax.numpy as jnp
from jax import lax
from jax.sharding import PartitionSpec as P

STEPS = 4
HALO = 4
nonlinear = 0.03
viscous = 0.02


def extended(shard, sides, width):
    for axis, dim in sides:
        count, length = (lax.axis_size(axis), shard.shape[dim])
        up = [(i, (i + 1) % count) for i in range(count - 1)]
        down = [(j, i) for i, j in up]
        last = lax.slice_in_dim(shard, length - width, length, axis=dim)
        first = lax.slice_in_dim(shard, 0, width, axis=dim)
        before = lax.ppermute(last, axis, up)
        after = lax.ppermute(first, axis, down)
        shard = jnp.concatenate([before, shard, after], axis=dim)
    return shard


def laplace(padded):
    middle = padded[1:-1, 1:-1, 1:-1]
    summed = padded[2:, 1:-1, 1:-1] + padded[:-2, 1:-1, 1:-1]
    summed = summed + padded[1:-1, 2:, 1:-1] + padded[1:-1, :-2, 1:-1]
    summed = summed + padded[1:-1, 1:-1, 2:] + padded[1:-1, 1:-1, :-2]
    return summed - 6.0 * middle


def advance(wide_now, wide_before, coefficient):
    current = wide_now[1:-1, 1:-1, 1:-1]
    before = wide_before[1:-1, 1:-1, 1:-1]
    change = current - before
    driving = (
        coefficient * laplace(wide_now)
        + viscous * laplace(wide_now - wide_before)
        + 2.0 * nonlinear * change * change
    )
    return 2.0 * current - before + (1.0 + 2.0 * nonlinear * current) * driving


def routing(owners, live_count, tile_total):
    slot_total = owners.shape[0]
    bucket = slot_total // tile_total
    position = jnp.arange(slot_total, dtype=jnp.int32)
    is_live = position < live_count
    member = (
        (owners[:, None] == jnp.arange(tile_total, dtype=jnp.int32)[None, :]) & is_live[:, None]
    ).astype(jnp.float32)
    earlier = (position[None, :] < position[:, None]).astype(jnp.float32)
    before = jnp.dot(earlier, member, precision=lax.Precision.HIGHEST)
    bucket_rank = jnp.sum(before * member, axis=1).astype(jnp.int32)
    target = owners * bucket + bucket_rank
    return ((target[:, None] == position[None, :]) & is_live[:, None]).astype(jnp.bfloat16)


def oscillate(forces, frequency, damping_ratio, start_state):

    def advance_mode(carried, force_row):
        displace, velocity = carried
        acceleration = (
            force_row
            - 2.0 * damping_ratio * frequency * velocity
            - frequency * frequency * displace
        )
        velocity = velocity + acceleration
        displace = displace + velocity
        return ((displace, velocity), acceleration)

    (displace, velocity), modal_accel = lax.scan(
        advance_mode, (start_state[0], start_state[1]), forces
    )
    return (modal_accel, jnp.stack([displace, velocity]))


def trim_rim(array, depth):
    return array[
        depth : array.shape[0] - depth,
        depth : array.shape[1] - depth,
        depth : array.shape[2] - depth,
    ]


def inside_range(offset, length, axis_devices, margin):
    position = offset * length - margin + jnp.arange(length + 2 * margin, dtype=jnp.int32)
    return ((position >= 0) & (position < axis_devices * length)).astype(jnp.float32)


def body(
    pressure,
    previous_pressure,
    courant_square,
    node_area,
    mode_shapes,
    frequency,
    damping_ratio,
    modal_start,
    slot_cell,
    slot_owner,
    surface_count,
):
    tile_total = lax.axis_size("tile")
    extent_first, extent_second, extent_third = pressure.shape
    slot_total = slot_cell.shape[-1]
    bucket = slot_total // tile_total
    routing_matrix = routing(slot_owner.reshape(slot_total), surface_count.reshape(()), tile_total)
    cell_index = slot_cell.reshape(slot_total)
    fields = jnp.stack([pressure, previous_pressure])
    margin = HALO
    coef_wide = extended(courant_square, (("tile", 0), ("sub", 1), ("rep", 2)), margin)
    inside_first = inside_range(lax.axis_index("tile"), extent_first, lax.axis_size("tile"), margin)
    inside_second = inside_range(lax.axis_index("sub"), extent_second, lax.axis_size("sub"), margin)
    inside_third = inside_range(lax.axis_index("rep"), extent_third, lax.axis_size("rep"), margin)
    inside = (
        inside_first[:, None, None] * inside_second[None, :, None] * inside_third[None, None, :]
    )

    def deep_block(carried, unused):
        padded = extended(carried, (("tile", 1), ("sub", 2), ("rep", 3)), margin)
        recorded = []
        for layer_index in range(margin):
            edge_depth = layer_index + 1
            updated = advance(padded[0], padded[1], trim_rim(coef_wide, edge_depth)) * trim_rim(
                inside, edge_depth
            )
            interior = trim_rim(updated, margin - edge_depth)
            recorded.append(jnp.take(interior.reshape(-1), cell_index).astype(jnp.bfloat16))
            padded = jnp.stack([updated, trim_rim(padded[0], 1)])
        return (padded, jnp.stack(recorded))

    fields, history = lax.scan(deep_block, fields, None, length=STEPS // margin)
    history = history.reshape(STEPS, slot_total)
    final_field = fields[0]
    prior_field = fields[1]
    bucketed = jnp.dot(history, routing_matrix, preferred_element_type=jnp.float32).astype(
        jnp.bfloat16
    )
    bucketed = bucketed.reshape(STEPS, tile_total, bucket)
    arrived = lax.all_to_all(bucketed, "tile", split_axis=1, concat_axis=1, tiled=True)
    arrived_flat = arrived.reshape(arrived.shape[0], slot_total)
    weighted = (arrived_flat * node_area).astype(jnp.bfloat16)
    partial_forces = jnp.dot(weighted, mode_shapes, preferred_element_type=jnp.float32)
    device_total = lax.axis_size("tile") * lax.axis_size("sub") * lax.axis_size("rep")
    mode_count = mode_shapes.shape[1]
    mode_share = mode_count // device_total
    first_mode = lax.axis_index(("tile", "sub", "rep")) * mode_share
    forces = lax.psum_scatter(
        partial_forces, ("tile", "sub", "rep"), scatter_dimension=1, tiled=True
    )
    local_frequency = lax.dynamic_slice_in_dim(frequency, first_mode, mode_share, 0)
    local_damping = lax.dynamic_slice_in_dim(damping_ratio, first_mode, mode_share, 0)
    local_start = lax.dynamic_slice_in_dim(modal_start, first_mode, mode_share, 1)
    modal_accel, modal_state = oscillate(forces, local_frequency, local_damping, local_start)
    modal_rounded = modal_accel.astype(jnp.bfloat16)
    node_accel = lax.dot_general(
        lax.all_gather(modal_rounded, ("tile", "sub", "rep"), axis=1, tiled=True),
        mode_shapes,
        (((1,), (1,)), ((), ())),
        preferred_element_type=jnp.float32,
    )
    outgoing = node_accel.astype(jnp.bfloat16).reshape(STEPS, tile_total, bucket)
    returned = lax.all_to_all(outgoing, "tile", split_axis=1, concat_axis=1, tiled=True)
    surface = lax.dot_general(
        returned.reshape(STEPS, slot_total),
        routing_matrix,
        (((1,), (1,)), ((), ())),
        preferred_element_type=jnp.float32,
    )
    surface_accel = surface.astype(jnp.bfloat16).reshape(1, 1, 1, STEPS, slot_total)
    return (final_field, prior_field, surface_accel, modal_state)


def solution(mesh):
    in_specs = (
        P(("groups", "tile"), "sub", "rep"),
        P(("groups", "tile"), "sub", "rep"),
        P(("groups", "tile"), "sub", "rep"),
        P(("groups", "tile", "sub", "rep")),
        P(("groups", "tile", "sub", "rep"), None),
        P("groups"),
        P("groups"),
        P(None, "groups"),
        P(("groups", "tile"), "sub", "rep", None),
        P(("groups", "tile"), "sub", "rep", None, None),
        P(("groups", "sub"), "rep", "tile"),
    )
    out_specs = (
        P(("groups", "tile"), "sub", "rep"),
        P(("groups", "tile"), "sub", "rep"),
        P(("groups", "tile"), "sub", "rep", None, None),
        P(None, ("groups", "tile", "sub", "rep")),
    )
    return jax.shard_map(body, mesh=mesh, in_specs=in_specs, out_specs=out_specs, check_vma=False)
```

profile of v0, /device:TPU:0, one launch (start us, length us, event | category | flops | bytes accessed | tf_op | source)
XLA Modules:
  0.0 172.1 jit_solution(446253793117891918)
XLA Ops:
  7.2 0.9 fusion.41
  8.1 5.0 %collective-permute-start = (f32[2,4,16,128]{3,2,1,0:T(8,128)S(1)}, f32[2,4,16,128]{3,2,1,0:T(8,128)S(1)}, u32[]{:S(2)}, u32[]{:S(2)}) collective-permute-start(f32[2,4,16,128]{3,2,1,0:T(8,128)S(1)} %get-tuple-element.142), channel_id=1, source_target_pairs={{0,4},{4,8},{8,12},{1,5},{5,9},{9,13},{2,6},{6,10},{10,14},{3,7},{... | collective-permute-start | bytes 196616 | tf_op jit(solution)/shard_map/while/body/eval_jaxpr/ppermute | solution.py:19
  13.1 1.3 collective-permute-start.1
  14.4 0.8 fusion.70
  15.2 4.5 %collective-permute-start.6 = (f32[4,16,128]{2,1,0:T(8,128)S(1)}, f32[4,16,128]{2,1,0:T(8,128)S(1)}, u32[]{:S(2)}, u32[]{:S(2)}) collective-permute-start(f32[4,16,128]{2,1,0:T(8,128)S(1)} %get-tuple-element.145), channel_id=1, source_target_pairs={{0,4},{4,8},{8,12},{1,5},{5,9},{9,13},{2,6},{6,10},{10,14},{3,7},{... | collective-permute-start | bytes 98312 | tf_op jit(solution)/shard_map/ppermute | solution.py:19
  19.7 1.3 collective-permute-start.7
  21.1 0.7 reduce
  22.5 0.7 reduce.1
  23.2 0.2 fusion.1
  23.4 0.1 broadcast_multiply_fusion.1
  23.5 0.1 broadcast_multiply_fusion
  23.6 0.7 constant_dynamic-slice_fusion
  24.3 0.8 constant_dynamic-update-slice_fusion.1
  25.1 0.4 collective-permute-done.7
  25.6 3.4 %collective-permute-start.8 = (f32[16,4,128]{2,1,0:T(4,128)S(1)}, f32[16,4,128]{2,1,0:T(4,128)S(1)}, u32[]{:S(2)}, u32[]{:S(2)}) collective-permute-start(f32[16,4,128]{2,1,0:T(4,128)S(1)} %get-tuple-element.140), channel_id=1, source_target_pairs={{0,2},{1,3},{4,6},{5,7},{8,10},{9,11},{12,14},{13,15},{16,18},{17,... | collective-permute-start | bytes 98312 | tf_op jit(solution)/shard_map/ppermute | solution.py:19
  29.0 1.3 collective-permute-start.9
  30.3 0.8 pad_maximum_fusion.7
  31.1 4.5 %collective-permute-start.2 = (f32[2,16,4,128]{3,2,1,0:T(4,128)S(1)}, f32[2,16,4,128]{3,2,1,0:T(4,128)S(1)}, u32[]{:S(2)}, u32[]{:S(2)}) collective-permute-start(f32[2,16,4,128]{3,2,1,0:T(4,128)S(1)} %get-tuple-element.136), channel_id=1, source_target_pairs={{0,2},{1,3},{4,6},{5,7},{8,10},{9,11},{12,14},{13,15},{16,18},{17,... | collective-permute-start | bytes 196616 | tf_op jit(solution)/shard_map/while/body/eval_jaxpr/ppermute | solution.py:19
  35.7 1.3 collective-permute-start.3
  37.1 0.1 fusion.68
  37.2 1.3 collective-permute-start.10
  38.5 1.3 collective-permute-start.11
  39.8 2.1 %collective-permute-done.3 = f32[2,16,4,128]{3,2,1,0:T(4,128)S(1)} collective-permute-done((f32[2,16,4,128]{3,2,1,0:T(4,128)S(1)}, f32[2,16,4,128]{3,2,1,0:T(4,128)S(1)}, u32[]{:S(2)}, u32[]{:S(2)}) %collective-permute-start.3) | collective-permute-done | bytes 65568 | tf_op jit(solution)/shard_map/while/body/eval_jaxpr/ppermute | solution.py:20
  41.9 0.1 pad_maximum_fusion.1
  41.9 0.2 fusion.67
  42.1 1.3 collective-permute-start.4
  43.4 1.3 collective-permute-start.5
  44.7 0.3 pad_maximum_fusion.2
  45.1 2.0 %collective-permute-done.5 = f32[2,16,24,4]{3,2,1,0:T(8,128)S(1)} collective-permute-done((f32[2,16,24,4]{3,2,1,0:T(8,128)S(1)}, f32[2,16,24,4]{3,2,1,0:T(8,128)S(1)}, u32[]{:S(2)}, u32[]{:S(2)}) %collective-permute-start.5) | collective-permute-done | bytes 12320 | tf_op jit(solution)/shard_map/while/body/eval_jaxpr/ppermute | solution.py:20
  47.0 0.5 pad_maximum_fusion
  47.6 0.1 slice_bitcast_fusion
  47.6 0.1 fusion.60
  47.7 1.4 slice_subtract_fusion
  49.1 0.1 slice.514
  49.2 1.2 slice_subtract_fusion.1
  50.4 0.1 slice.499
  50.5 1.0 slice_subtract_fusion.2
  51.6 0.3 fusion.40
  51.9 2.5 %gather_fusion.2 = bf16[384]{0:T(512)(128)(2,1)S(1)} fusion(f32[16384]{0:T(1024)S(1)} %bitcast.42, s32[1024]{0:T(1024)S(1)} %pad_clamp_fusion), kind=kCustom, calls=%fused_computation.2.clone | custom fusion | bytes 3072 | tf_op jit(solution)/shard_map/while/body/eval_jaxpr/jit(_take)/gather | solution.py:130
  54.5 2.5 %gather_fusion.3 = bf16[384]{0:T(512)(128)(2,1)S(1)} fusion(f32[16384]{0:T(1024)S(1)} %bitcast.41, s32[1024]{0:T(1024)S(1)} %pad_clamp_fusion), kind=kCustom, calls=%fused_computation.3.clone | custom fusion | bytes 3072 | tf_op jit(solution)/shard_map/while/body/eval_jaxpr/jit(_take)/gather | solution.py:130
  57.0 2.8 %gather_fusion.1 = bf16[384]{0:T(512)(128)(2,1)S(1)} fusion(bf16[16384]{0:T(1024)(128)(2,1)S(1)} %bitcast.40, s32[1024]{0:T(1024)S(1)} %pad_clamp_fusion), kind=kCustom, calls=%fused_computation.1.clone | custom fusion | bytes 3072 | tf_op jit(solution)/shard_map/while/body/eval_jaxpr/jit(_take)/gather | solution.py:130
  59.9 2.8 %gather_fusion = bf16[384]{0:T(512)(128)(2,1)S(1)} fusion(bf16[16384]{0:T(1024)(128)(2,1)S(1)} %bitcast.39, s32[1024]{0:T(1024)S(1)} %pad_clamp_fusion), kind=kCustom, calls=%fused_computation.clone | custom fusion | bytes 3072 | tf_op jit(solution)/shard_map/while/body/eval_jaxpr/jit(_take)/gather | solution.py:130
  62.8 0.3 convolution_convert_fusion.1
  63.1 0.1 reshape.135
  63.1 0.6 copy.17
  63.7 5.5 %all-to-all-start = ((bf16[4,4,96]{2,0,1:T(4,128)(2,1)}), bf16[4,4,96]{2,0,1:T(4,128)(2,1)S(1)}, u32[]{:S(2)}, u32[]{:S(2)}) async-start(bf16[4,4,96]{2,0,1:T(4,128)(2,1)} %copy.17), calls=%async_computation | async-start | bytes 8192 | tf_op jit(solution)/shard_map/all_to_all | solution.py:142
  69.3 5.6 %all-to-all-done = bf16[4,4,96]{2,0,1:T(4,128)(2,1)S(1)} async-done(((bf16[4,4,96]{2,0,1:T(4,128)(2,1)}), bf16[4,4,96]{2,0,1:T(4,128)(2,1)S(1)}, u32[]{:S(2)}, u32[]{:S(2)}) %all-to-all-start) | async-done | bytes 3104 | tf_op jit(solution)/shard_map/all_to_all | solution.py:142
  74.9 0.1 reshape.139
  75.0 1.7 %convolution_bitcast_fusion = f32[2048,4]{1,0:T(8,128)} fusion(bf16[384,2048]{1,0:T(8,128)(2,1)S(1)} %copy-done, f32[4,384]{1,0:T(4,128)S(1)} %reshape.139, f32[384]{0:T(512)S(1)} %copy-done.6), kind=kOutput, calls=%fused_computation.6 | convolution fusion | flops 6294528 | bytes 1613312
  76.7 0.0 reduce-scatter.4.cloned.1.call-update
  76.7 0.8 fusion.63
  77.5 0.8 dynamic_slice.15
  78.3 55.4 %reduce-scatter.4.cloned.1.call-done = f32[128,4]{1,0:T(8,128)} async-done(((f32[2048,4]{1,0:T(8,128)}), f32[128,4]{1,0:T(8,128)}) %reduce-scatter.4.cloned.1.call-update) | async-done | bytes 2064
  133.7 0.9 copy.22
  134.6 0.3 while.4
  134.9 19.4 %all_gather.3 = bf16[4,2048]{1,0:T(4,128)(2,1)S(1)} all-gather(bf16[4,128]{1,0:T(4,128)(2,1)S(1)} %get-tuple-element.98), channel_id=1, replica_groups=mesh['groups'=2,'tile'=4,'sub'=2,'rep'=2] {'tile','sub','rep'}, dimensions={1}, use_global_device_ids=true | all-gather | bytes 17408 | tf_op jit(solution)/shard_map/all_gather | solution.py:159
  154.2 0.5 convolution_convert_fusion.2
  154.8 0.1 reshape.136
  154.8 0.6 copy.19
  155.5 3.2 %all-to-all-start.1 = ((bf16[4,4,96]{2,0,1:T(4,128)(2,1)}), bf16[4,4,96]{2,0,1:T(4,128)(2,1)S(1)}, u32[]{:S(2)}, u32[]{:S(2)}) async-start(bf16[4,4,96]{2,0,1:T(4,128)(2,1)} %copy.19), calls=%async_computation.1 | async-start | bytes 8192 | tf_op jit(solution)/shard_map/all_to_all | solution.py:165
  158.7 0.6 pad_maximum_fusion.9
  159.3 5.0 %all-to-all-done.1 = bf16[4,4,96]{2,0,1:T(4,128)(2,1)S(1)} async-done(((bf16[4,4,96]{2,0,1:T(4,128)(2,1)}), bf16[4,4,96]{2,0,1:T(4,128)(2,1)S(1)}, u32[]{:S(2)}, u32[]{:S(2)}) %all-to-all-start.1) | async-done | bytes 3104 | tf_op jit(solution)/shard_map/all_to_all | solution.py:165
  164.3 0.1 reshape.137
  164.4 0.9 fusion.2
  (53 shorter events, 0.5 us)
Async XLA Ops:
  7.2 67.8 %copy-start = (bf16[384,2048]{1,0:T(8,128)(2,1)S(1)}, bf16[384,2048]{1,0:T(8,128)(2,1)}, u32[]{:S(2)}) copy-start(bf16[384,2048]{1,0:T(8,128)(2,1)} %param.19) | copy-start | bytes 4718596
  7.2 34.7 %copy-start.3 = (f32[8,16,128]{2,1,0:T(8,128)S(1)}, f32[8,16,128]{2,1,0:T(8,128)}, u32[]{:S(2)}) copy-start(f32[8,16,128]{2,1,0:T(8,128)} %param.15) | copy-start | bytes 196612
  7.2 34.7 %copy-start.4 = (f32[8,16,128]{2,1,0:T(8,128)S(1)}, f32[8,16,128]{2,1,0:T(8,128)}, u32[]{:S(2)}) copy-start(f32[8,16,128]{2,1,0:T(8,128)} %param.16) | copy-start | bytes 196612
  8.1 22.1 %collective-permute-start = (f32[2,4,16,128]{3,2,1,0:T(8,128)S(1)}, f32[2,4,16,128]{3,2,1,0:T(8,128)S(1)}, u32[]{:S(2)}, u32[]{:S(2)}) collective-permute-start(f32[2,4,16,128]{3,2,1,0:T(8,128)S(1)} %get-tuple-element.142), channel_id=1, source_target_pairs={{0,4},{4,8},{8,12},{1,5},{5,9},{9,13},{2,6},{6,10},{10,14},{3,7},{... | collective-permute-start | bytes 196616 | tf_op jit(solution)/shard_map/while/body/eval_jaxpr/ppermute | solution.py:19
  13.1 17.2 %collective-permute-start.1 = (f32[2,4,16,128]{3,2,1,0:T(8,128)S(1)}, f32[2,4,16,128]{3,2,1,0:T(8,128)S(1)}, u32[]{:S(2)}, u32[]{:S(2)}) collective-permute-start(f32[2,4,16,128]{3,2,1,0:T(8,128)S(1)} %get-tuple-element.143), channel_id=1, source_target_pairs={{4,0},{8,4},{12,8},{5,1},{9,5},{13,9},{6,2},{10,6},{14,10},{7,3},{... | collective-permute-start | bytes 196616 | tf_op jit(solution)/shard_map/while/body/eval_jaxpr/ppermute | solution.py:20
  15.2 9.1 %collective-permute-start.6 = (f32[4,16,128]{2,1,0:T(8,128)S(1)}, f32[4,16,128]{2,1,0:T(8,128)S(1)}, u32[]{:S(2)}, u32[]{:S(2)}) collective-permute-start(f32[4,16,128]{2,1,0:T(8,128)S(1)} %get-tuple-element.145), channel_id=1, source_target_pairs={{0,4},{4,8},{8,12},{1,5},{5,9},{9,13},{2,6},{6,10},{10,14},{3,7},{... | collective-permute-start | bytes 98312 | tf_op jit(solution)/shard_map/ppermute | solution.py:19
  19.7 5.8 %collective-permute-start.7 = (f32[4,16,128]{2,1,0:T(8,128)S(1)}, f32[4,16,128]{2,1,0:T(8,128)S(1)}, u32[]{:S(2)}, u32[]{:S(2)}) collective-permute-start(f32[4,16,128]{2,1,0:T(8,128)S(1)} %get-tuple-element.144), channel_id=1, source_target_pairs={{4,0},{8,4},{12,8},{5,1},{9,5},{13,9},{6,2},{10,6},{14,10},{7,3},{... | collective-permute-start | bytes 98312 | tf_op jit(solution)/shard_map/ppermute | solution.py:20
  25.6 11.4 %collective-permute-start.8 = (f32[16,4,128]{2,1,0:T(4,128)S(1)}, f32[16,4,128]{2,1,0:T(4,128)S(1)}, u32[]{:S(2)}, u32[]{:S(2)}) collective-permute-start(f32[16,4,128]{2,1,0:T(4,128)S(1)} %get-tuple-element.140), channel_id=1, source_target_pairs={{0,2},{1,3},{4,6},{5,7},{8,10},{9,11},{12,14},{13,15},{16,18},{17,... | collective-permute-start | bytes 98312 | tf_op jit(solution)/shard_map/ppermute | solution.py:19
  29.0 8.0 %collective-permute-start.9 = (f32[16,4,128]{2,1,0:T(4,128)S(1)}, f32[16,4,128]{2,1,0:T(4,128)S(1)}, u32[]{:S(2)}, u32[]{:S(2)}) collective-permute-start(f32[16,4,128]{2,1,0:T(4,128)S(1)} %get-tuple-element.141), channel_id=1, source_target_pairs={{2,0},{3,1},{6,4},{7,5},{10,8},{11,9},{14,12},{15,13},{18,16},{19,... | collective-permute-start | bytes 98312 | tf_op jit(solution)/shard_map/ppermute | solution.py:20
  31.1 8.6 %collective-permute-start.2 = (f32[2,16,4,128]{3,2,1,0:T(4,128)S(1)}, f32[2,16,4,128]{3,2,1,0:T(4,128)S(1)}, u32[]{:S(2)}, u32[]{:S(2)}) collective-permute-start(f32[2,16,4,128]{3,2,1,0:T(4,128)S(1)} %get-tuple-element.136), channel_id=1, source_target_pairs={{0,2},{1,3},{4,6},{5,7},{8,10},{9,11},{12,14},{13,15},{16,18},{17,... | collective-permute-start | bytes 196616 | tf_op jit(solution)/shard_map/while/body/eval_jaxpr/ppermute | solution.py:19
  35.7 6.2 %collective-permute-start.3 = (f32[2,16,4,128]{3,2,1,0:T(4,128)S(1)}, f32[2,16,4,128]{3,2,1,0:T(4,128)S(1)}, u32[]{:S(2)}, u32[]{:S(2)}) collective-permute-start(f32[2,16,4,128]{3,2,1,0:T(4,128)S(1)} %get-tuple-element.137), channel_id=1, source_target_pairs={{2,0},{3,1},{6,4},{7,5},{10,8},{11,9},{14,12},{15,13},{18,16},{19,... | collective-permute-start | bytes 196616 | tf_op jit(solution)/shard_map/while/body/eval_jaxpr/ppermute | solution.py:20
  37.2 7.6 %collective-permute-start.10 = (f32[16,24,4]{2,1,0:T(8,128)S(1)}, f32[16,24,4]{2,1,0:T(8,128)S(1)}, u32[]{:S(2)}, u32[]{:S(2)}) collective-permute-start(f32[16,24,4]{2,1,0:T(8,128)S(1)} %get-tuple-element.138), channel_id=1, source_target_pairs={{0,1},{2,3},{4,5},{6,7},{8,9},{10,11},{12,13},{14,15},{16,17},{18,... | collective-permute-start | bytes 18440 | tf_op jit(solution)/shard_map/ppermute | solution.py:19
  38.5 6.3 %collective-permute-start.11 = (f32[16,24,4]{2,1,0:T(8,128)S(1)}, f32[16,24,4]{2,1,0:T(8,128)S(1)}, u32[]{:S(2)}, u32[]{:S(2)}) collective-permute-start(f32[16,24,4]{2,1,0:T(8,128)S(1)} %get-tuple-element.139), channel_id=1, source_target_pairs={{1,0},{3,2},{5,4},{7,6},{9,8},{11,10},{13,12},{15,14},{17,16},{19,... | collective-permute-start | bytes 18440 | tf_op jit(solution)/shard_map/ppermute | solution.py:20
  42.1 2.9 %collective-permute-start.4 = (f32[2,16,24,4]{3,2,1,0:T(8,128)S(1)}, f32[2,16,24,4]{3,2,1,0:T(8,128)S(1)}, u32[]{:S(2)}, u32[]{:S(2)}) collective-permute-start(f32[2,16,24,4]{3,2,1,0:T(8,128)S(1)} %get-tuple-element.134), channel_id=1, source_target_pairs={{0,1},{2,3},{4,5},{6,7},{8,9},{10,11},{12,13},{14,15},{16,17},{18,... | collective-permute-start | bytes 36872 | tf_op jit(solution)/shard_map/while/body/eval_jaxpr/ppermute | solution.py:19
  43.4 3.6 %collective-permute-start.5 = (f32[2,16,24,4]{3,2,1,0:T(8,128)S(1)}, f32[2,16,24,4]{3,2,1,0:T(8,128)S(1)}, u32[]{:S(2)}, u32[]{:S(2)}) collective-permute-start(f32[2,16,24,4]{3,2,1,0:T(8,128)S(1)} %get-tuple-element.135), channel_id=1, source_target_pairs={{1,0},{3,2},{5,4},{7,6},{9,8},{11,10},{13,12},{15,14},{17,16},{19,... | collective-permute-start | bytes 36872 | tf_op jit(solution)/shard_map/while/body/eval_jaxpr/ppermute | solution.py:20
  50.5 1.1 copy-start.5
  51.9 7.9 %copy-start.1 = (f32[8,16,128]{2,1,0:T(8,128)}, f32[8,16,128]{2,1,0:T(8,128)S(1)}, u32[]{:S(2)}) copy-start(f32[8,16,128]{2,1,0:T(8,128)S(1)} %get-tuple-element.124) | copy-start | bytes 196612
  51.9 7.9 %copy-start.2 = (f32[8,16,128]{2,1,0:T(8,128)}, f32[8,16,128]{2,1,0:T(8,128)S(1)}, u32[]{:S(2)}) copy-start(f32[8,16,128]{2,1,0:T(8,128)S(1)} %get-tuple-element.125) | copy-start | bytes 196612
  54.5 20.5 %copy-start.6 = (f32[384]{0:T(512)S(1)}, f32[384]{0:T(512)}, u32[]{:S(2)}) copy-start(f32[384]{0:T(512)} %param.18) | copy-start | bytes 4612
  63.7 11.1 %all-to-all-start = ((bf16[4,4,96]{2,0,1:T(4,128)(2,1)}), bf16[4,4,96]{2,0,1:T(4,128)(2,1)S(1)}, u32[]{:S(2)}, u32[]{:S(2)}) async-start(bf16[4,4,96]{2,0,1:T(4,128)(2,1)} %copy.17), calls=%async_computation | async-start | bytes 8192 | tf_op jit(solution)/shard_map/all_to_all | solution.py:142
  69.3 64.4 %reduce-scatter.4.cloned.1.call-start = ((), (), s32[]{:S(2)}) async-start(), calls=%async_computation.3 | async-start | bytes 1114112
  155.5 8.8 %all-to-all-start.1 = ((bf16[4,4,96]{2,0,1:T(4,128)(2,1)}), bf16[4,4,96]{2,0,1:T(4,128)(2,1)S(1)}, u32[]{:S(2)}, u32[]{:S(2)}) async-start(bf16[4,4,96]{2,0,1:T(4,128)(2,1)} %copy.19), calls=%async_computation.1 | async-start | bytes 8192 | tf_op jit(solution)/shard_map/all_to_all | solution.py:165
Sparse Core Ops, SparseCore 0:
  76.9 56.7 reduce-scatter.3
where the time goes:
time: 173 us; the launch traced here: 172 us
  waiting for transfers between devices  70.5 us (41%)
  starting transfers between devices  36.6 us (21%)
  blocking collectives  19.4 us (11%)
  local copies, waits for them, and re-layouts  17 us (10%)
  between operations  15.2 us (9%)
  other arithmetic  9.79 us (6%)
  matrix products  3.65 us (2%)
    unnamed x2, waiting for transfers between devices  55.5 us
    ppermute x6, starting transfers between devices, extended(): before = lax.ppermute(last, axis, up)  20.1 us
    all_gather x1, blocking collectives, body(): lax.all_gather(modal_rounded, ('tile', 'sub', 'rep'), axis=1, tiled=True)  19.4 us
    gather x4, local copies, waits for them, and re-layouts, deep_block(): jnp.take(interior.reshape(-1), cell_index).astype(jnp.bfloat16)  10.7 us
    ppermute x6, starting transfers between devices, extended(): after = lax.ppermute(first, axis, down)  7.75 us
    all_to_all x1, waiting for transfers between devices, body(): lax.all_to_all(bucketed, 'tile', split_axis=1, concat_axis=1, tiled=True)  5.57 us
    all_to_all x1, starting transfers between devices, body(): lax.all_to_all(bucketed, 'tile', split_axis=1, concat_axis=1, tiled=True)  5.54 us
    all_to_all x1, waiting for transfers between devices, body(): lax.all_to_all(outgoing, 'tile', split_axis=1, concat_axis=1, tiled=True)  4.98 us
  transfers between devices with their start and end apart: 15, of which 6 were waited for; matrix products, arithmetic and copies ran while one was open for 5% of the time, Pallas kernels for 0%

commit v1 on v0

--- a/solution.py
+++ b/solution.py
@@ -156,7 +156,15 @@
     modal_accel, modal_state = oscillate(forces, local_frequency, local_damping, local_start)
     modal_rounded = modal_accel.astype(jnp.bfloat16)
     node_accel = lax.dot_general(
-        lax.all_gather(modal_rounded, ("tile", "sub", "rep"), axis=1, tiled=True),
+        jnp.concatenate(
+            lax.all_to_all(
+                jnp.stack([modal_rounded] * lax.axis_size(("tile", "sub", "rep"))),
+                ("tile", "sub", "rep"),
+                0,
+                0,
+            ),
+            axis=1,
+        ),
         mode_shapes,
         (((1,), (1,)), ((), ())),
         preferred_element_type=jnp.float32,

time: 173 us -> 164 us (0.948)
  blocking collectives: 19.4 us -> 10 us
    all_gather x1 -> x0, blocking collectives: 19.4 us -> none  [body(): lax.all_gather(modal_rounded, ('tile', 'sub', 'rep'), axis=1, tiled=True)]
    all_to_all x0 -> x1, blocking collectives: none -> 10 us  [body(): lax.all_to_all(jnp.stack([modal_rounded] * lax.axis_size(('tile', 'sub',...]
where the time goes in v1:
time: 164 us; the launch traced here: 163 us
  waiting for transfers between devices  70.5 us (43%)
  starting transfers between devices  36.6 us (22%)
  local copies, waits for them, and re-layouts  17 us (10%)
  between operations  15.2 us (9%)
  blocking collectives  10 us (6%)
  other arithmetic  9.79 us (6%)
  matrix products  3.65 us (2%)
    unnamed x2, waiting for transfers between devices  55.5 us
    ppermute x6, starting transfers between devices, extended(): before = lax.ppermute(last, axis, up)  20.1 us
    gather x4, local copies, waits for them, and re-layouts, deep_block(): jnp.take(interior.reshape(-1), cell_index).astype(jnp.bfloat16)  10.7 us
    all_to_all x1, blocking collectives, body(): lax.all_to_all(jnp.stack([modal_rounded] * lax.axis_size(('tile', 'sub',...  10 us
    ppermute x6, starting transfers between devices, extended(): after = lax.ppermute(first, axis, down)  7.75 us
    all_to_all x1, waiting for transfers between devices, body(): lax.all_to_all(bucketed, 'tile', split_axis=1, concat_axis=1, tiled=True)  5.57 us
    all_to_all x1, starting transfers between devices, body(): lax.all_to_all(bucketed, 'tile', split_axis=1, concat_axis=1, tiled=True)  5.54 us
    all_to_all x1, waiting for transfers between devices, body(): lax.all_to_all(outgoing, 'tile', split_axis=1, concat_axis=1, tiled=True)  4.98 us
  transfers between devices with their start and end apart: 15, of which 6 were waited for; matrix products, arithmetic and copies ran while one was open for 5% of the time, Pallas kernels for 0%

profile of v1, /device:TPU:0, one launch (start us, length us, event | category | flops | bytes accessed | tf_op | source)
XLA Modules:
  0.0 162.8 jit_solution(3236139979904960050)
XLA Ops:
  7.2 0.9 fusion.41
  8.1 5.0 %collective-permute-start = (f32[2,4,16,128]{3,2,1,0:T(8,128)S(1)}, f32[2,4,16,128]{3,2,1,0:T(8,128)S(1)}, u32[]{:S(2)}, u32[]{:S(2)}) collective-permute-start(f32[2,4,16,128]{3,2,1,0:T(8,128)S(1)} %get-tuple-element.142), channel_id=1, source_target_pairs={{0,4},{4,8},{8,12},{1,5},{5,9},{9,13},{2,6},{6,10},{10,14},{3,7},{... | collective-permute-start | bytes 196616 | tf_op jit(solution)/shard_map/while/body/eval_jaxpr/ppermute | solution.py:19
  13.1 1.3 collective-permute-start.1
  14.4 0.8 fusion.71
  15.2 4.5 %collective-permute-start.6 = (f32[4,16,128]{2,1,0:T(8,128)S(1)}, f32[4,16,128]{2,1,0:T(8,128)S(1)}, u32[]{:S(2)}, u32[]{:S(2)}) collective-permute-start(f32[4,16,128]{2,1,0:T(8,128)S(1)} %get-tuple-element.145), channel_id=1, source_target_pairs={{0,4},{4,8},{8,12},{1,5},{5,9},{9,13},{2,6},{6,10},{10,14},{3,7},{... | collective-permute-start | bytes 98312 | tf_op jit(solution)/shard_map/ppermute | solution.py:19
  19.7 1.3 collective-permute-start.7
  21.1 0.7 reduce
  22.5 0.7 reduce.1
  23.2 0.2 fusion.1
  23.4 0.1 broadcast_multiply_fusion.1
  23.5 0.1 broadcast_multiply_fusion
  23.6 0.7 constant_dynamic-slice_fusion
  24.3 0.8 constant_dynamic-update-slice_fusion.1
  25.1 0.4 collective-permute-done.7
  25.6 3.4 %collective-permute-start.8 = (f32[16,4,128]{2,1,0:T(4,128)S(1)}, f32[16,4,128]{2,1,0:T(4,128)S(1)}, u32[]{:S(2)}, u32[]{:S(2)}) collective-permute-start(f32[16,4,128]{2,1,0:T(4,128)S(1)} %get-tuple-element.140), channel_id=1, source_target_pairs={{0,2},{1,3},{4,6},{5,7},{8,10},{9,11},{12,14},{13,15},{16,18},{17,... | collective-permute-start | bytes 98312 | tf_op jit(solution)/shard_map/ppermute | solution.py:19
  29.0 1.3 collective-permute-start.9
  30.3 0.8 pad_maximum_fusion.7
  31.1 4.5 %collective-permute-start.2 = (f32[2,16,4,128]{3,2,1,0:T(4,128)S(1)}, f32[2,16,4,128]{3,2,1,0:T(4,128)S(1)}, u32[]{:S(2)}, u32[]{:S(2)}) collective-permute-start(f32[2,16,4,128]{3,2,1,0:T(4,128)S(1)} %get-tuple-element.136), channel_id=1, source_target_pairs={{0,2},{1,3},{4,6},{5,7},{8,10},{9,11},{12,14},{13,15},{16,18},{17,... | collective-permute-start | bytes 196616 | tf_op jit(solution)/shard_map/while/body/eval_jaxpr/ppermute | solution.py:19
  35.7 1.3 collective-permute-start.3
  37.1 0.1 fusion.69
  37.2 1.3 collective-permute-start.10
  38.5 1.3 collective-permute-start.11
  39.8 2.1 %collective-permute-done.3 = f32[2,16,4,128]{3,2,1,0:T(4,128)S(1)} collective-permute-done((f32[2,16,4,128]{3,2,1,0:T(4,128)S(1)}, f32[2,16,4,128]{3,2,1,0:T(4,128)S(1)}, u32[]{:S(2)}, u32[]{:S(2)}) %collective-permute-start.3) | collective-permute-done | bytes 65568 | tf_op jit(solution)/shard_map/while/body/eval_jaxpr/ppermute | solution.py:20
  41.9 0.1 pad_maximum_fusion.1
  41.9 0.2 fusion.68
  42.1 1.3 collective-permute-start.4
  43.4 1.3 collective-permute-start.5
  44.7 0.3 pad_maximum_fusion.2
  45.1 2.0 %collective-permute-done.5 = f32[2,16,24,4]{3,2,1,0:T(8,128)S(1)} collective-permute-done((f32[2,16,24,4]{3,2,1,0:T(8,128)S(1)}, f32[2,16,24,4]{3,2,1,0:T(8,128)S(1)}, u32[]{:S(2)}, u32[]{:S(2)}) %collective-permute-start.5) | collective-permute-done | bytes 12320 | tf_op jit(solution)/shard_map/while/body/eval_jaxpr/ppermute | solution.py:20
  47.0 0.5 pad_maximum_fusion
  47.6 0.1 slice_bitcast_fusion
  47.6 0.1 fusion.61
  47.7 1.4 slice_subtract_fusion
  49.1 0.1 slice.514
  49.2 1.2 slice_subtract_fusion.1
  50.4 0.1 slice.499
  50.5 1.0 slice_subtract_fusion.2
  51.6 0.3 fusion.40
  51.9 2.5 %gather_fusion.2 = bf16[384]{0:T(512)(128)(2,1)S(1)} fusion(f32[16384]{0:T(1024)S(1)} %bitcast.46, s32[1024]{0:T(1024)S(1)} %pad_clamp_fusion), kind=kCustom, calls=%fused_computation.2.clone | custom fusion | bytes 3072 | tf_op jit(solution)/shard_map/while/body/eval_jaxpr/jit(_take)/gather | solution.py:130
  54.5 2.5 %gather_fusion.3 = bf16[384]{0:T(512)(128)(2,1)S(1)} fusion(f32[16384]{0:T(1024)S(1)} %bitcast.45, s32[1024]{0:T(1024)S(1)} %pad_clamp_fusion), kind=kCustom, calls=%fused_computation.3.clone | custom fusion | bytes 3072 | tf_op jit(solution)/shard_map/while/body/eval_jaxpr/jit(_take)/gather | solution.py:130
  57.0 2.8 %gather_fusion.1 = bf16[384]{0:T(512)(128)(2,1)S(1)} fusion(bf16[16384]{0:T(1024)(128)(2,1)S(1)} %bitcast.44, s32[1024]{0:T(1024)S(1)} %pad_clamp_fusion), kind=kCustom, calls=%fused_computation.1.clone | custom fusion | bytes 3072 | tf_op jit(solution)/shard_map/while/body/eval_jaxpr/jit(_take)/gather | solution.py:130
  59.9 2.8 %gather_fusion = bf16[384]{0:T(512)(128)(2,1)S(1)} fusion(bf16[16384]{0:T(1024)(128)(2,1)S(1)} %bitcast.43, s32[1024]{0:T(1024)S(1)} %pad_clamp_fusion), kind=kCustom, calls=%fused_computation.clone | custom fusion | bytes 3072 | tf_op jit(solution)/shard_map/while/body/eval_jaxpr/jit(_take)/gather | solution.py:130
  62.8 0.3 convolution_convert_fusion.1
  63.1 0.1 reshape.143
  63.1 0.6 copy.17
  63.7 5.5 %all-to-all-start = ((bf16[4,4,96]{2,0,1:T(4,128)(2,1)}), bf16[4,4,96]{2,0,1:T(4,128)(2,1)S(1)}, u32[]{:S(2)}, u32[]{:S(2)}) async-start(bf16[4,4,96]{2,0,1:T(4,128)(2,1)} %copy.17), calls=%async_computation | async-start | bytes 8192 | tf_op jit(solution)/shard_map/all_to_all | solution.py:142
  69.3 5.6 %all-to-all-done = bf16[4,4,96]{2,0,1:T(4,128)(2,1)S(1)} async-done(((bf16[4,4,96]{2,0,1:T(4,128)(2,1)}), bf16[4,4,96]{2,0,1:T(4,128)(2,1)S(1)}, u32[]{:S(2)}, u32[]{:S(2)}) %all-to-all-start) | async-done | bytes 3104 | tf_op jit(solution)/shard_map/all_to_all | solution.py:142
  74.9 0.1 reshape.149
  75.0 1.7 %convolution_bitcast_fusion = f32[2048,4]{1,0:T(8,128)} fusion(bf16[384,2048]{1,0:T(8,128)(2,1)S(1)} %copy-done, f32[4,384]{1,0:T(4,128)S(1)} %reshape.149, f32[384]{0:T(512)S(1)} %copy-done.6), kind=kOutput, calls=%fused_computation.6 | convolution fusion | flops 6294528 | bytes 1613312
  76.7 0.0 reduce-scatter.4.cloned.1.call-update
  76.7 0.8 fusion.64
  77.5 0.8 dynamic_slice.15
  78.3 55.4 %reduce-scatter.4.cloned.1.call-done = f32[128,4]{1,0:T(8,128)} async-done(((f32[2048,4]{1,0:T(8,128)}), f32[128,4]{1,0:T(8,128)}) %reduce-scatter.4.cloned.1.call-update) | async-done | bytes 2064
  133.7 0.9 copy.22
  134.6 0.3 while.4
  134.9 10.0 %all_to_all.15 = bf16[16,4,128]{2,1,0:T(4,128)(2,1)S(1)} all-to-all(bf16[16,4,128]{2,1,0:T(4,128)(2,1)S(1)} %stack.71), channel_id=1, replica_groups=mesh['groups'=2,'tile'=4,'sub'=2,'rep'=2] {'tile','sub','rep'}, dimensions={0} | all-to-all | bytes 32768 | tf_op jit(solution)/shard_map/all_to_all | solution.py:160
  144.9 0.5 convolution_convert_fusion.2
  145.4 0.1 reshape.146
  145.5 0.6 copy.19
  146.1 3.2 %all-to-all-start.2 = ((bf16[4,4,96]{2,0,1:T(4,128)(2,1)}), bf16[4,4,96]{2,0,1:T(4,128)(2,1)S(1)}, u32[]{:S(2)}, u32[]{:S(2)}) async-start(bf16[4,4,96]{2,0,1:T(4,128)(2,1)} %copy.19), calls=%async_computation.2 | async-start | bytes 8192 | tf_op jit(solution)/shard_map/all_to_all | solution.py:173
  149.4 0.6 pad_maximum_fusion.9
  150.0 5.0 %all-to-all-done.2 = bf16[4,4,96]{2,0,1:T(4,128)(2,1)S(1)} async-done(((bf16[4,4,96]{2,0,1:T(4,128)(2,1)}), bf16[4,4,96]{2,0,1:T(4,128)(2,1)S(1)}, u32[]{:S(2)}, u32[]{:S(2)}) %all-to-all-start.2) | async-done | bytes 3104 | tf_op jit(solution)/shard_map/all_to_all | solution.py:173
  154.9 0.1 reshape.147
  155.0 0.9 fusion.2
  (54 shorter events, 0.5 us)
Async XLA Ops:
  7.2 67.8 %copy-start = (bf16[384,2048]{1,0:T(8,128)(2,1)S(1)}, bf16[384,2048]{1,0:T(8,128)(2,1)}, u32[]{:S(2)}) copy-start(bf16[384,2048]{1,0:T(8,128)(2,1)} %param.19) | copy-start | bytes 4718596
  7.2 34.7 %copy-start.3 = (f32[8,16,128]{2,1,0:T(8,128)S(1)}, f32[8,16,128]{2,1,0:T(8,128)}, u32[]{:S(2)}) copy-start(f32[8,16,128]{2,1,0:T(8,128)} %param.15) | copy-start | bytes 196612
  7.2 34.7 %copy-start.4 = (f32[8,16,128]{2,1,0:T(8,128)S(1)}, f32[8,16,128]{2,1,0:T(8,128)}, u32[]{:S(2)}) copy-start(f32[8,16,128]{2,1,0:T(8,128)} %param.16) | copy-start | bytes 196612
  8.1 22.1 %collective-permute-start = (f32[2,4,16,128]{3,2,1,0:T(8,128)S(1)}, f32[2,4,16,128]{3,2,1,0:T(8,128)S(1)}, u32[]{:S(2)}, u32[]{:S(2)}) collective-permute-start(f32[2,4,16,128]{3,2,1,0:T(8,128)S(1)} %get-tuple-element.142), channel_id=1, source_target_pairs={{0,4},{4,8},{8,12},{1,5},{5,9},{9,13},{2,6},{6,10},{10,14},{3,7},{... | collective-permute-start | bytes 196616 | tf_op jit(solution)/shard_map/while/body/eval_jaxpr/ppermute | solution.py:19
  13.1 17.2 %collective-permute-start.1 = (f32[2,4,16,128]{3,2,1,0:T(8,128)S(1)}, f32[2,4,16,128]{3,2,1,0:T(8,128)S(1)}, u32[]{:S(2)}, u32[]{:S(2)}) collective-permute-start(f32[2,4,16,128]{3,2,1,0:T(8,128)S(1)} %get-tuple-element.143), channel_id=1, source_target_pairs={{4,0},{8,4},{12,8},{5,1},{9,5},{13,9},{6,2},{10,6},{14,10},{7,3},{... | collective-permute-start | bytes 196616 | tf_op jit(solution)/shard_map/while/body/eval_jaxpr/ppermute | solution.py:20
  15.2 9.1 %collective-permute-start.6 = (f32[4,16,128]{2,1,0:T(8,128)S(1)}, f32[4,16,128]{2,1,0:T(8,128)S(1)}, u32[]{:S(2)}, u32[]{:S(2)}) collective-permute-start(f32[4,16,128]{2,1,0:T(8,128)S(1)} %get-tuple-element.145), channel_id=1, source_target_pairs={{0,4},{4,8},{8,12},{1,5},{5,9},{9,13},{2,6},{6,10},{10,14},{3,7},{... | collective-permute-start | bytes 98312 | tf_op jit(solution)/shard_map/ppermute | solution.py:19
  19.7 5.8 %collective-permute-start.7 = (f32[4,16,128]{2,1,0:T(8,128)S(1)}, f32[4,16,128]{2,1,0:T(8,128)S(1)}, u32[]{:S(2)}, u32[]{:S(2)}) collective-permute-start(f32[4,16,128]{2,1,0:T(8,128)S(1)} %get-tuple-element.144), channel_id=1, source_target_pairs={{4,0},{8,4},{12,8},{5,1},{9,5},{13,9},{6,2},{10,6},{14,10},{7,3},{... | collective-permute-start | bytes 98312 | tf_op jit(solution)/shard_map/ppermute | solution.py:20
  25.6 11.4 %collective-permute-start.8 = (f32[16,4,128]{2,1,0:T(4,128)S(1)}, f32[16,4,128]{2,1,0:T(4,128)S(1)}, u32[]{:S(2)}, u32[]{:S(2)}) collective-permute-start(f32[16,4,128]{2,1,0:T(4,128)S(1)} %get-tuple-element.140), channel_id=1, source_target_pairs={{0,2},{1,3},{4,6},{5,7},{8,10},{9,11},{12,14},{13,15},{16,18},{17,... | collective-permute-start | bytes 98312 | tf_op jit(solution)/shard_map/ppermute | solution.py:19
  29.0 8.0 %collective-permute-start.9 = (f32[16,4,128]{2,1,0:T(4,128)S(1)}, f32[16,4,128]{2,1,0:T(4,128)S(1)}, u32[]{:S(2)}, u32[]{:S(2)}) collective-permute-start(f32[16,4,128]{2,1,0:T(4,128)S(1)} %get-tuple-element.141), channel_id=1, source_target_pairs={{2,0},{3,1},{6,4},{7,5},{10,8},{11,9},{14,12},{15,13},{18,16},{19,... | collective-permute-start | bytes 98312 | tf_op jit(solution)/shard_map/ppermute | solution.py:20
  31.1 8.6 %collective-permute-start.2 = (f32[2,16,4,128]{3,2,1,0:T(4,128)S(1)}, f32[2,16,4,128]{3,2,1,0:T(4,128)S(1)}, u32[]{:S(2)}, u32[]{:S(2)}) collective-permute-start(f32[2,16,4,128]{3,2,1,0:T(4,128)S(1)} %get-tuple-element.136), channel_id=1, source_target_pairs={{0,2},{1,3},{4,6},{5,7},{8,10},{9,11},{12,14},{13,15},{16,18},{17,... | collective-permute-start | bytes 196616 | tf_op jit(solution)/shard_map/while/body/eval_jaxpr/ppermute | solution.py:19
  35.7 6.2 %collective-permute-start.3 = (f32[2,16,4,128]{3,2,1,0:T(4,128)S(1)}, f32[2,16,4,128]{3,2,1,0:T(4,128)S(1)}, u32[]{:S(2)}, u32[]{:S(2)}) collective-permute-start(f32[2,16,4,128]{3,2,1,0:T(4,128)S(1)} %get-tuple-element.137), channel_id=1, source_target_pairs={{2,0},{3,1},{6,4},{7,5},{10,8},{11,9},{14,12},{15,13},{18,16},{19,... | collective-permute-start | bytes 196616 | tf_op jit(solution)/shard_map/while/body/eval_jaxpr/ppermute | solution.py:20
  37.2 7.6 %collective-permute-start.10 = (f32[16,24,4]{2,1,0:T(8,128)S(1)}, f32[16,24,4]{2,1,0:T(8,128)S(1)}, u32[]{:S(2)}, u32[]{:S(2)}) collective-permute-start(f32[16,24,4]{2,1,0:T(8,128)S(1)} %get-tuple-element.138), channel_id=1, source_target_pairs={{0,1},{2,3},{4,5},{6,7},{8,9},{10,11},{12,13},{14,15},{16,17},{18,... | collective-permute-start | bytes 18440 | tf_op jit(solution)/shard_map/ppermute | solution.py:19
  38.5 6.3 %collective-permute-start.11 = (f32[16,24,4]{2,1,0:T(8,128)S(1)}, f32[16,24,4]{2,1,0:T(8,128)S(1)}, u32[]{:S(2)}, u32[]{:S(2)}) collective-permute-start(f32[16,24,4]{2,1,0:T(8,128)S(1)} %get-tuple-element.139), channel_id=1, source_target_pairs={{1,0},{3,2},{5,4},{7,6},{9,8},{11,10},{13,12},{15,14},{17,16},{19,... | collective-permute-start | bytes 18440 | tf_op jit(solution)/shard_map/ppermute | solution.py:20
  42.1 2.9 %collective-permute-start.4 = (f32[2,16,24,4]{3,2,1,0:T(8,128)S(1)}, f32[2,16,24,4]{3,2,1,0:T(8,128)S(1)}, u32[]{:S(2)}, u32[]{:S(2)}) collective-permute-start(f32[2,16,24,4]{3,2,1,0:T(8,128)S(1)} %get-tuple-element.134), channel_id=1, source_target_pairs={{0,1},{2,3},{4,5},{6,7},{8,9},{10,11},{12,13},{14,15},{16,17},{18,... | collective-permute-start | bytes 36872 | tf_op jit(solution)/shard_map/while/body/eval_jaxpr/ppermute | solution.py:19
  43.4 3.6 %collective-permute-start.5 = (f32[2,16,24,4]{3,2,1,0:T(8,128)S(1)}, f32[2,16,24,4]{3,2,1,0:T(8,128)S(1)}, u32[]{:S(2)}, u32[]{:S(2)}) collective-permute-start(f32[2,16,24,4]{3,2,1,0:T(8,128)S(1)} %get-tuple-element.135), channel_id=1, source_target_pairs={{1,0},{3,2},{5,4},{7,6},{9,8},{11,10},{13,12},{15,14},{17,16},{19,... | collective-permute-start | bytes 36872 | tf_op jit(solution)/shard_map/while/body/eval_jaxpr/ppermute | solution.py:20
  50.5 1.1 copy-start.5
  51.9 7.9 %copy-start.1 = (f32[8,16,128]{2,1,0:T(8,128)}, f32[8,16,128]{2,1,0:T(8,128)S(1)}, u32[]{:S(2)}) copy-start(f32[8,16,128]{2,1,0:T(8,128)S(1)} %get-tuple-element.124) | copy-start | bytes 196612
  51.9 7.9 %copy-start.2 = (f32[8,16,128]{2,1,0:T(8,128)}, f32[8,16,128]{2,1,0:T(8,128)S(1)}, u32[]{:S(2)}) copy-start(f32[8,16,128]{2,1,0:T(8,128)S(1)} %get-tuple-element.125) | copy-start | bytes 196612
  54.5 20.5 %copy-start.6 = (f32[384]{0:T(512)S(1)}, f32[384]{0:T(512)}, u32[]{:S(2)}) copy-start(f32[384]{0:T(512)} %param.18) | copy-start | bytes 4612
  63.7 11.1 %all-to-all-start = ((bf16[4,4,96]{2,0,1:T(4,128)(2,1)}), bf16[4,4,96]{2,0,1:T(4,128)(2,1)S(1)}, u32[]{:S(2)}, u32[]{:S(2)}) async-start(bf16[4,4,96]{2,0,1:T(4,128)(2,1)} %copy.17), calls=%async_computation | async-start | bytes 8192 | tf_op jit(solution)/shard_map/all_to_all | solution.py:142
  69.3 64.4 %reduce-scatter.4.cloned.1.call-start = ((), (), s32[]{:S(2)}) async-start(), calls=%async_computation.4 | async-start | bytes 1114112
  146.1 8.8 %all-to-all-start.2 = ((bf16[4,4,96]{2,0,1:T(4,128)(2,1)}), bf16[4,4,96]{2,0,1:T(4,128)(2,1)S(1)}, u32[]{:S(2)}, u32[]{:S(2)}) async-start(bf16[4,4,96]{2,0,1:T(4,128)(2,1)} %copy.19), calls=%async_computation.2 | async-start | bytes 8192 | tf_op jit(solution)/shard_map/all_to_all | solution.py:173
Sparse Core Ops, SparseCore 0:
  76.9 56.7 reduce-scatter.3
